TPU v7x, 32 devices: a whole 2x2x4 slice. The times are simulated.
32 devices in a mesh: row: 4 (over z), col: 8 (over y, x, core).
Axes of the slice: x: 2, y: 2, z: 4, core: 2. Of those that a mesh axis runs over, the one named last changes fastest.
Arguments:
- hamiltonian: bfloat16 [2048, 2048], P('row', 'col'), may hold values from -0.3 to 0.3
- pattern: int32 [16, 16], replicated, may hold values from 0 to 1, as said below
- tile_lists: int32 [32, 8], replicated, may hold values from 0 to 15, as said below
- orders: int32 [32], replicated, may hold values from 6 to 8
- shift: float32 [1], replicated, may hold values from -0.5 to 0.5
Outputs:
- density: bfloat16 [2048, 2048], P('row', 'col')
- php: float32 [2048, 2048], P('row', 'col')
Inputs may be any that keep to these rules, and one draw needn't show every extreme that they name: `pattern`: Symmetric, with zeros on the diagonal. `tile_lists`: row s begins with tile s * 64 // 128; its entries lie in distinct groups of 2 consecutive tiles, and the second lies in the group that shares a group of 4 consecutive tiles with the first. Entries from position orders[s] on are not used.
All inputs are finite; a program needn't handle non-finite values.
Results may differ from a plain program's by a relative error of at most 0.0073.
Values may be sent and summed in bfloat16 or wider, within the bound.
A program may use at most 64 MiB of HBM per device.

v0:
```python
import jax
import jax.numpy as jnp
from jax import lax
from jax.sharding import PartitionSpec as P

TILE = 128
TPC = 2
MAXT = 8
ITERS = 3


def newton_density(sub, live_rows, potential):
    eye = jnp.eye(sub.shape[0], dtype=jnp.float32)
    shifted = sub.astype(jnp.float32) - potential * eye * live_rows[None, :]
    row_squares = jnp.sum(shifted * shifted, axis=1)
    scale = jnp.abs(potential) + 2.0 * jnp.sqrt(jnp.max(row_squares) + 1e-06)
    iterate = (shifted / scale).astype(jnp.bfloat16)
    product = shifted
    for step in range(ITERS):
        square = jnp.dot(iterate, iterate, preferred_element_type=jnp.float32)
        factor = (1.5 * eye - 0.5 * square).astype(jnp.bfloat16)
        product = jnp.dot(iterate, factor, preferred_element_type=jnp.float32)
        if step + 1 < ITERS:
            iterate = product.astype(jnp.bfloat16)
    return 0.5 * (eye - product)


def per_device(hamiltonian, pattern, tile_lists, orders, shift):
    rows_n = lax.axis_size("row")
    cols_n = lax.axis_size("col")
    devices = rows_n * cols_n
    me_row = lax.axis_index("row")
    me_col = lax.axis_index("col")
    solver = me_row * cols_n + me_col
    count = pattern.shape[0]
    row_tiles = count // rows_n
    width = TPC * TILE // rows_n
    pairs = MAXT * MAXT
    steps = jnp.arange(MAXT, dtype=jnp.int32)
    keep = jnp.maximum(pattern, jnp.eye(count, dtype=jnp.int32))
    local_keep = lax.dynamic_slice(keep, (me_row * row_tiles, me_col * TPC), (row_tiles, TPC))
    full_keep = jnp.repeat(jnp.repeat(local_keep, TILE, axis=0), TILE, axis=1)
    masked = jnp.where(full_keep > 0, hamiltonian, jnp.zeros_like(hamiltonian))
    blocks = (
        masked.reshape(row_tiles, TILE, TPC, TILE)
        .transpose(0, 2, 1, 3)
        .reshape(row_tiles * TPC, TILE, TILE)
    )
    live_all = steps[None, :] < orders[:, None]
    owned = (tile_lists[:, :, None] // row_tiles == me_row) & (
        tile_lists[:, None, :] // TPC == me_col
    )
    owned = owned & live_all[:, :, None] & live_all[:, None, :]
    owned = owned.reshape(devices, pairs)
    rank = jnp.cumsum(owned.astype(jnp.int32), axis=1) - 1
    local_index = (
        (tile_lists[:, :, None] - me_row * row_tiles) * TPC
        + (tile_lists[:, None, :] - me_col * TPC)
    ).reshape(devices, pairs)
    slots = []
    for slot in range(2):
        pick = owned & (rank == slot)
        found = jnp.any(pick, axis=1)
        which = jnp.sum(jnp.where(pick, local_index, 0), axis=1)
        picked = jnp.take(blocks, which, axis=0)
        slots.append(jnp.where(found[:, None, None], picked, jnp.zeros_like(picked)))
    outgoing = jnp.stack(slots, axis=1)
    arrived = lax.all_to_all(outgoing, ("row", "col"), split_axis=0, concat_axis=0, tiled=True)
    arrived = arrived.reshape(devices * 2, TILE, TILE)
    mine = lax.dynamic_index_in_dim(tile_lists, solver, 0, keepdims=False)
    order_here = lax.dynamic_index_in_dim(orders, solver, 0, keepdims=False)
    live = steps < order_here
    both = (live[:, None] & live[None, :]).reshape(pairs)
    owner = (mine[:, None] // row_tiles * cols_n + mine[None, :] // TPC).reshape(pairs)
    flat_pairs = jnp.arange(pairs, dtype=jnp.int32)
    earlier = (
        (owner[:, None] == owner[None, :])
        & both[None, :]
        & (flat_pairs[None, :] < flat_pairs[:, None])
    )
    slot_of = jnp.sum(earlier.astype(jnp.int32), axis=1)
    source = jnp.where(both, owner * 2 + slot_of, 0)
    sub = jnp.take(arrived, source, axis=0)
    sub = jnp.where(both[:, None, None], sub, jnp.zeros_like(sub))
    sub = (
        sub.reshape(MAXT, MAXT, TILE, TILE).transpose(0, 2, 1, 3).reshape(MAXT * TILE, MAXT * TILE)
    )
    live_rows = jnp.repeat(live.astype(jnp.float32), TILE)
    dens = newton_density(sub, live_rows, shift[0])
    offset = solver * width % TILE
    central = lax.dynamic_slice_in_dim(dens, offset, width, 1).astype(jnp.bfloat16)
    central = central.reshape(MAXT, TILE, width).transpose(0, 2, 1)
    home_col = solver * width // (TPC * TILE)
    groups = mine // row_tiles
    ahead = (groups[:, None] == groups[None, :]) & live[None, :] & (steps[None, :] < steps[:, None])
    place = jnp.sum(ahead.astype(jnp.int32), axis=1)
    target = groups * cols_n + home_col
    chooser = jnp.arange(devices, dtype=jnp.int32)[:, None, None] == target[None, None, :]
    chooser = (
        chooser
        & (jnp.arange(2, dtype=jnp.int32)[None, :, None] == place[None, None, :])
        & live[None, None, :]
    )
    back = jnp.einsum(
        "dki,iwt->dkwt", chooser.astype(jnp.bfloat16), central, preferred_element_type=jnp.float32
    ).astype(jnp.bfloat16)
    returned = lax.all_to_all(back, ("row", "col"), split_axis=0, concat_axis=0, tiled=True)
    returned = returned.reshape(devices * 2, width, TILE)
    homes = lax.dynamic_slice_in_dim(tile_lists, me_col * rows_n, rows_n, 0)
    home_orders = lax.dynamic_slice_in_dim(orders, me_col * rows_n, rows_n, 0)
    home_live = steps[None, :] < home_orders[:, None]
    home_groups = homes // row_tiles
    home_ahead = (
        (home_groups[:, :, None] == home_groups[:, None, :])
        & home_live[:, None, :]
        & (steps[None, None, :] < steps[None, :, None])
    )
    home_place = jnp.sum(home_ahead.astype(jnp.int32), axis=2)
    local_rows = me_row * row_tiles + jnp.arange(row_tiles, dtype=jnp.int32)
    hit = (homes[None, :, :] == local_rows[:, None, None]) & home_live[None, :, :]
    found = jnp.any(hit, axis=2)
    slot_here = jnp.sum(jnp.where(hit, home_place[None, :, :], 0), axis=2)
    sub_index = me_col * rows_n + jnp.arange(rows_n, dtype=jnp.int32)
    flat_index = jnp.where(found, sub_index[None, :] * 2 + slot_here, 0)
    pieces = jnp.take(returned, flat_index.reshape(-1), axis=0).reshape(
        row_tiles, rows_n, width, TILE
    )
    pieces = jnp.where(found[:, :, None, None], pieces, jnp.zeros_like(pieces))
    density = pieces.transpose(0, 3, 1, 2).reshape(row_tiles * TILE, rows_n * width)
    p_strip = lax.all_gather(density, "row", axis=0, tiled=True)
    part = p_strip
    hp = jnp.dot(
        lax.all_gather(masked, "col", axis=1, tiled=True), part, preferred_element_type=jnp.float32
    ).astype(jnp.bfloat16)
    q_strip = lax.all_gather(hp, "row", axis=0, tiled=True)
    part = q_strip
    php = jnp.dot(
        lax.all_gather(density, "col", axis=1, tiled=True), part, preferred_element_type=jnp.float32
    )
    return (density, php)


def solution(mesh):
    in_specs = (P("row", "col"), P(), P(), P(), P())
    out_specs = (P("row", "col"), P("row", "col"))
    return jax.shard_map(
        per_device, mesh=mesh, in_specs=in_specs, out_specs=out_specs, check_vma=False
    )
```

profile of v0, /device:TPU:0, one launch (start us, length us, event | category | flops | bytes accessed | tf_op | source)
XLA Modules:
  0.0 244.3 jit_solution(1091136820264881119)
XLA Ops:
  11.0 1.1 copy.77
  14.6 1.5 copy.81
  16.1 7.3 %all-to-all-start = ((bf16[32,2,128,128]{3,2,1,0:T(8,128)(2,1)}), bf16[32,2,128,128]{3,2,1,0:T(8,128)(2,1)S(1)}, u32[]{:S(2)}, u32[]{:S(2)}) async-start(bf16[32,2,128,128]{3,2,1,0:T(8,128)(2,1)} %copy.81), calls=%async_computation | async-start | bytes 4194304 | tf_op jit(solution)/shard_map/all_to_all | solution.py:68
  28.5 43.7 %all-to-all-done = bf16[32,2,128,128]{3,2,1,0:T(8,128)(2,1)S(1)} async-done(((bf16[32,2,128,128]{3,2,1,0:T(8,128)(2,1)}), bf16[32,2,128,128]{3,2,1,0:T(8,128)(2,1)S(1)}, u32[]{:S(2)}, u32[]{:S(2)}) %all-to-all-start) | async-done | bytes 2097184 | tf_op jit(solution)/shard_map/all_to_all | solution.py:68
  72.2 1.3 copy-done.1
  73.5 2.5 %gather_fusion = bf16[64,128,128]{2,1,0:T(8,128)(2,1)S(1)} fusion(bf16[64,128,128]{2,1,0:T(8,128)(2,1)} %bitcast.105, s32[1024]{0:T(1024)S(1)} %pad_clamp_fusion.1), kind=kCustom, calls=%fused_computation.2 | custom fusion | bytes 4194560 | tf_op jit(solution)/shard_map/jit(_take)/gather | solution.py:83
  76.1 2.4 convert_bitcast_fusion
  78.5 1.7 multiply_reduce_fusion
  81.5 1.8 divide_convert_fusion
  83.3 1.4 copy.83
  84.7 4.3 %copy.82 = f32[8,128,8,128]{3,2,1,0:T(8,128)} copy(f32[8,128,8,128]{3,1,2,0:T(8,128)S(1)} %copy-done) | data formatting | bytes 8388608 | tf_op jit(solution)/shard_map/convert_element_type | solution.py:14
  89.0 8.2 %fusion.9 = bf16[1024,1024]{1,0:T(8,128)(2,1)} fusion(f32[128,8,8,128]{3,2,1,0:T(8,128)} %bitcast.106, f32[]{:T(128)S(6)} %add.284, f32[1024]{0:T(1024)S(1)} %broadcast_bitcast_fusion, f32[]{:T(128)} %bitcast.98, bf16[128,8,8,128]{3,2,1,0:T(8,128)(2,1)S(1)} %bitcast.110), kind=kOutput, calls=%fused_computation.23 | convolution fusion | flops 4307550208 | bytes 8392712 | tf_op jit(solution)/shard_map/dot_general | solution.py:22
  97.1 7.5 %convolution_convert_fusion = bf16[1024,1024]{1,0:T(8,128)(2,1)S(1)} fusion(bf16[1024,1024]{1,0:T(8,128)(2,1)} %fusion.9), kind=kOutput, calls=%fused_computation.24 | convolution fusion | flops 4301258752 | bytes 4194304 | tf_op jit(solution)/shard_map/dot_general | solution.py:22
  104.7 6.6 %fusion.16 = f32[1024,1024]{1,0:T(8,128)} fusion(bf16[1024,1024]{1,0:T(8,128)(2,1)S(1)} %convolution_convert_fusion), kind=kOutput, calls=%fused_computation.31 | convolution fusion | flops 4300210176 | bytes 6291456 | tf_op jit(solution)/shard_map/dot_general | solution.py:22
  111.3 1.4 fusion.18
  113.4 1.4 copy.86
  114.8 4.1 %all-to-all-start.1 = ((bf16[32,2,64,128]{3,2,1,0:T(8,128)(2,1)}), bf16[32,2,64,128]{3,2,1,0:T(8,128)(2,1)S(1)}, u32[]{:S(2)}, u32[]{:S(2)}) async-start(bf16[32,2,64,128]{3,2,1,0:T(8,128)(2,1)} %copy.86), calls=%async_computation.1 | async-start | bytes 2097152 | tf_op jit(solution)/shard_map/all_to_all | solution.py:107
  120.2 25.0 %all-to-all-done.1 = bf16[32,2,64,128]{3,2,1,0:T(8,128)(2,1)S(1)} async-done(((bf16[32,2,64,128]{3,2,1,0:T(8,128)(2,1)}), bf16[32,2,64,128]{3,2,1,0:T(8,128)(2,1)S(1)}, u32[]{:S(2)}, u32[]{:S(2)}) %all-to-all-start.1) | async-done | bytes 1048608 | tf_op jit(solution)/shard_map/all_to_all | solution.py:107
  146.9 27.1 %all-gather.9.cloned.1.call-done = bf16[2048,256]{0,1:T(8,128)(2,1)} async-done(((bf16[512,256]{0,1:T(8,128)(2,1)}), bf16[2048,256]{0,1:T(8,128)(2,1)}) %all-gather.9.cloned.1.call-update) | async-done | bytes 1048592 | tf_op jit(solution)/shard_map/all_gather | solution.py:130
  174.0 3.3 %convolution_convert_fusion.2 = bf16[512,256]{1,0:T(8,128)(2,1)} fusion(bf16[512,2048]{0,1:T(8,128)(2,1)} %all-gather.7.cloned.1.call-done, bf16[2048,256]{0,1:T(8,128)(2,1)} %all-gather.9.cloned.1.call-done), kind=kOutput, calls=%fused_computation.26 | convolution fusion | flops 537001984 | bytes 3407872 | tf_op jit(solution)/shard_map/dot_general | solution.py:132
  177.9 0.8 copy.88
  178.8 26.1 %all-gather.11.cloned.1.call-done = bf16[2048,256]{1,0:T(8,128)(2,1)} async-done(((bf16[512,256]{1,0:T(8,128)(2,1)}), bf16[2048,256]{1,0:T(8,128)(2,1)}) %all-gather.11.cloned.1.call-update) | async-done | bytes 1048592 | tf_op jit(solution)/shard_map/all_gather | solution.py:135
  204.8 29.5 %all-gather.5.cloned.1.call-done = bf16[512,2048]{0,1:T(8,128)(2,1)} async-done(((bf16[512,256]{0,1:T(8,128)(2,1)}), bf16[512,2048]{0,1:T(8,128)(2,1)}) %all-gather.5.cloned.1.call-update) | async-done | bytes 2097168 | tf_op jit(solution)/shard_map/all_gather | solution.py:138
  234.3 3.4 %fusion.59 = f32[512,256]{1,0:T(8,128)} fusion(bf16[512,2048]{0,1:T(8,128)(2,1)} %all-gather.5.cloned.1.call-done, bf16[2048,256]{1,0:T(8,128)(2,1)} %all-gather.11.cloned.1.call-done), kind=kOutput, calls=%fused_computation.154 | convolution fusion | flops 536870912 | bytes 3670016 | tf_op jit(solution)/shard_map/dot_general | solution.py:137
  (91 shorter events, 15.3 us)
Async XLA Ops:
  12.1 2.3 copy-start.3
  14.6 9.6 %copy-start.5 = (s32[32]{0:T(128)S(1)}, s32[32]{0:T(128)}, u32[]{:S(2)}) copy-start(s32[32]{0:T(128)} %param.10) | copy-start | bytes 388
  14.6 11.1 %copy-start.4 = (s32[32,8]{0,1:T(8,128)S(1)}, s32[32,8]{0,1:T(8,128)}, u32[]{:S(2)}) copy-start(s32[32,8]{0,1:T(8,128)} %param.9) | copy-start | bytes 3076
  16.1 56.1 %all-to-all-start = ((bf16[32,2,128,128]{3,2,1,0:T(8,128)(2,1)}), bf16[32,2,128,128]{3,2,1,0:T(8,128)(2,1)S(1)}, u32[]{:S(2)}, u32[]{:S(2)}) async-start(bf16[32,2,128,128]{3,2,1,0:T(8,128)(2,1)} %copy.81), calls=%async_computation | async-start | bytes 4194304 | tf_op jit(solution)/shard_map/all_to_all | solution.py:68
  23.4 123.5 %all-gather.7.cloned.1.call-start = ((), (), s32[]{:S(2)}) async-start(), calls=%async_computation.3 | async-start | bytes 2359296 | tf_op jit(solution)/shard_map/all_gather | solution.py:133
  72.2 1.4 copy-start.1
  81.5 3.2 %copy-start = (f32[8,128,8,128]{3,1,2,0:T(8,128)S(1)}, f32[8,128,8,128]{3,1,2,0:T(8,128)}, u32[]{:S(2)}) copy-start(f32[8,128,8,128]{3,1,2,0:T(8,128)} %convert_bitcast_fusion) | copy-start | bytes 12582916
  114.8 30.3 %all-to-all-start.1 = ((bf16[32,2,64,128]{3,2,1,0:T(8,128)(2,1)}), bf16[32,2,64,128]{3,2,1,0:T(8,128)(2,1)S(1)}, u32[]{:S(2)}, u32[]{:S(2)}) async-start(bf16[32,2,64,128]{3,2,1,0:T(8,128)(2,1)} %copy.86), calls=%async_computation.1 | async-start | bytes 2097152 | tf_op jit(solution)/shard_map/all_to_all | solution.py:107
  118.9 55.1 %all-gather.9.cloned.1.call-start = ((), (), s32[]{:S(2)}) async-start(), calls=%async_computation.4 | async-start | bytes 1310720 | tf_op jit(solution)/shard_map/all_gather | solution.py:130
  146.8 31.1 %copy-start.2 = (bf16[32,8,4,128]{3,1,2,0:T(8,128)(2,1)S(1)}, bf16[32,8,4,128]{3,1,2,0:T(8,128)(2,1)}, u32[]{:S(2)}) copy-start(bf16[32,8,4,128]{3,1,2,0:T(8,128)(2,1)} %copy.107) | copy-start | bytes 786436
  146.8 58.0 %all-gather.11.cloned.1.call-start = ((), (), s32[]{:S(2)}) async-start(), calls=%async_computation.5 | async-start | bytes 1310720 | tf_op jit(solution)/shard_map/all_gather | solution.py:135
  177.3 57.0 %all-gather.5.cloned.1.call-start = ((), (), s32[]{:S(2)}) async-start(), calls=%async_computation.2 | async-start | bytes 2359296 | tf_op jit(solution)/shard_map/all_gather | solution.py:138
Sparse Core Ops, SparseCore 0:
  26.7 35.3 all-gather.6
  146.9 26.9 all-gather.8
  177.5 27.3 all-gather.10
  207.2 27.1 all-gather.4
where the time goes:
time: 245 us; the launch traced here: 244 us
  waiting for transfers between devices  153 us (62%)
  matrix products  29.6 us (12%)
  local copies, waits for them, and re-layouts  19.7 us (8%)
  between operations  15.6 us (6%)
  other arithmetic  15.3 us (6%)
  starting transfers between devices  11.6 us (5%)
    all_to_all x1, waiting for transfers between devices, per_device(): lax.all_to_all(outgoing, ('row', 'col'), split_axis=0, concat_axis=0, til...  43.7 us
    all_gather x1, waiting for transfers between devices, per_device(): lax.all_gather(density, 'col', axis=1, tiled=True)  29.5 us
    all_gather x1, waiting for transfers between devices, per_device(): p_strip = lax.all_gather(density, 'row', axis=0, tiled=True)  27.1 us
    all_gather x1, waiting for transfers between devices, per_device(): q_strip = lax.all_gather(hp, 'row', axis=0, tiled=True)  26.1 us
    all_to_all x1, waiting for transfers between devices, per_device(): lax.all_to_all(back, ('row', 'col'), split_axis=0, concat_axis=0, tiled=T...  25 us
    dot_general x3, matrix products, newton_density(): product = jnp.dot(iterate, factor, preferred_element_type=jnp.float32)  22.3 us
    all_to_all x1, starting transfers between devices, per_device(): lax.all_to_all(outgoing, ('row', 'col'), split_axis=0, concat_axis=0, til...  7.33 us
  transfers between devices with their start and end apart: 6, of which 5 were waited for; matrix products, arithmetic and copies ran while one was open for 20% of the time, Pallas kernels for 0%

commit v1 on v0

--- a/solution.py
+++ b/solution.py
@@ -132,7 +132,12 @@
     hp = jnp.dot(
         lax.all_gather(masked, "col", axis=1, tiled=True), part, preferred_element_type=jnp.float32
     ).astype(jnp.bfloat16)
-    q_strip = lax.all_gather(hp, "row", axis=0, tiled=True)
+    ring = [hp]
+    for hop in range(3):
+        ring.append(lax.ppermute(ring[-1], "row", [(dev, (dev + 1) % 4) for dev in range(4)]))
+    q_strip = jnp.roll(
+        jnp.concatenate(ring[::-1], axis=0), (lax.axis_index("row") + 1) * ring[0].shape[0], axis=0
+    )
     part = q_strip
     php = jnp.dot(
         lax.all_gather(density, "col", axis=1, tiled=True), part, preferred_element_type=jnp.float32

time: 245 us -> 220 us (0.90)
  waiting for transfers between devices: 153 us -> 120 us
  local copies, waits for them, and re-layouts: 19.7 us -> 26.4 us
    all_gather x1, waiting for transfers between devices: 29.5 us -> 0.01 us  [per_device(): lax.all_gather(density, 'col', axis=1, tiled=True)]
    all_gather x1 -> x0, waiting for transfers between devices: 26.1 us -> none  [per_device(): q_strip = lax.all_gather(hp, 'row', axis=0, tiled=True)]
    ppermute x0 -> x3, waiting for transfers between devices: none -> 23.8 us  [per_device(): lax.ppermute(ring[-1], 'row', [(dev, (dev + 1) % 4) for dev in range(4)])]
    unnamed x17 -> x24, local copies, waits for them, and re-layouts: 4.14 us -> 10 us
  transfers between devices with their start and end apart: 6 -> 8, of which waited for: 5 -> 6; matrix products, arithmetic and copies ran while one was open for 20% -> 26% of each run, Pallas kernels for 0% -> 0%
where the time goes in v1:
time: 220 us; the launch traced here: 219 us
  waiting for transfers between devices  120 us (55%)
  matrix products  28.9 us (13%)
  local copies, waits for them, and re-layouts  26.4 us (12%)
  between operations  15.5 us (7%)
  other arithmetic  15.3 us (7%)
  starting transfers between devices  13.1 us (6%)
    all_to_all x1, waiting for transfers between devices, per_device(): lax.all_to_all(outgoing, ('row', 'col'), split_axis=0, concat_axis=0, til...  43.7 us
    all_gather x1, waiting for transfers between devices, per_device(): p_strip = lax.all_gather(density, 'row', axis=0, tiled=True)  26.4 us
    all_to_all x1, waiting for transfers between devices, per_device(): lax.all_to_all(back, ('row', 'col'), split_axis=0, concat_axis=0, tiled=T...  25 us
    ppermute x3, waiting for transfers between devices, per_device(): lax.ppermute(ring[-1], 'row', [(dev, (dev + 1) % 4) for dev in range(4)])  23.8 us
    dot_general x3, matrix products, newton_density(): product = jnp.dot(iterate, factor, preferred_element_type=jnp.float32)  22.3 us
    unnamed x24, local copies, waits for them, and re-layouts  10 us
    all_to_all x1, starting transfers between devices, per_device(): lax.all_to_all(outgoing, ('row', 'col'), split_axis=0, concat_axis=0, til...  7.33 us
  transfers between devices with their start and end apart: 8, of which 6 were waited for; matrix products, arithmetic and copies ran while one was open for 26% of the time, Pallas kernels for 0%

profile of v1, /device:TPU:0, one launch (start us, length us, event | category | flops | bytes accessed | tf_op | source)
XLA Modules:
  0.0 219.3 jit_solution(7619980431018422989)
XLA Ops:
  14.6 1.6 copy.81
  16.2 7.3 %all-to-all-start = ((bf16[32,2,128,128]{3,2,1,0:T(8,128)(2,1)}), bf16[32,2,128,128]{3,2,1,0:T(8,128)(2,1)S(1)}, u32[]{:S(2)}, u32[]{:S(2)}) async-start(bf16[32,2,128,128]{3,2,1,0:T(8,128)(2,1)} %copy.81), calls=%async_computation | async-start | bytes 4194304 | tf_op jit(solution)/shard_map/all_to_all | solution.py:68
  28.6 43.7 %all-to-all-done = bf16[32,2,128,128]{3,2,1,0:T(8,128)(2,1)S(1)} async-done(((bf16[32,2,128,128]{3,2,1,0:T(8,128)(2,1)}), bf16[32,2,128,128]{3,2,1,0:T(8,128)(2,1)S(1)}, u32[]{:S(2)}, u32[]{:S(2)}) %all-to-all-start) | async-done | bytes 2097184 | tf_op jit(solution)/shard_map/all_to_all | solution.py:68
  72.3 1.3 copy-done.1
  73.6 2.5 %gather_fusion = bf16[64,128,128]{2,1,0:T(8,128)(2,1)S(1)} fusion(bf16[64,128,128]{2,1,0:T(8,128)(2,1)} %bitcast.104, s32[1024]{0:T(1024)S(1)} %pad_clamp_fusion.1), kind=kCustom, calls=%fused_computation.2 | custom fusion | bytes 4194560 | tf_op jit(solution)/shard_map/jit(_take)/gather | solution.py:83
  76.2 2.4 %convert_bitcast_fusion = f32[8,128,8,128]{3,1,2,0:T(8,128)} fusion(pred[8,8]{1,0:T(8,128)(4,1)S(1)} %compare_and_fusion.3, pred[8,8]{1,0:T(8,128)(4,1)S(1)} %broadcast_and_fusion, bf16[64,128,128]{2,1,0:T(8,128)(2,1)S(1)} %gather_fusion), kind=kLoop, calls=%fused_computation.13 | loop fusion | flops 3145728 | bytes 6291584 | tf_op jit(solution)/shard_map/convert_element_type | solution.py:14
  78.5 1.7 multiply_reduce_fusion
  81.6 1.8 divide_convert_fusion
  83.4 1.4 copy.83
  85.6 4.3 %copy.82 = f32[8,128,8,128]{3,2,1,0:T(8,128)} copy(f32[8,128,8,128]{3,1,2,0:T(8,128)S(1)} %copy-done) | data formatting | bytes 8388608 | tf_op jit(solution)/shard_map/convert_element_type | solution.py:14
  89.9 8.2 %fusion.9 = bf16[1024,1024]{1,0:T(8,128)(2,1)} fusion(f32[128,8,8,128]{3,2,1,0:T(8,128)} %bitcast.105, f32[]{:T(128)S(6)} %add.297, f32[1024]{0:T(1024)S(1)} %broadcast_bitcast_fusion, f32[]{:T(128)} %bitcast.97, bf16[128,8,8,128]{3,2,1,0:T(8,128)(2,1)S(1)} %bitcast.109), kind=kOutput, calls=%fused_computation.23 | convolution fusion | flops 4307550208 | bytes 8392712 | tf_op jit(solution)/shard_map/dot_general | solution.py:22
  98.0 7.5 %convolution_convert_fusion = bf16[1024,1024]{1,0:T(8,128)(2,1)S(1)} fusion(bf16[1024,1024]{1,0:T(8,128)(2,1)} %fusion.9), kind=kOutput, calls=%fused_computation.24 | convolution fusion | flops 4301258752 | bytes 4194304 | tf_op jit(solution)/shard_map/dot_general | solution.py:22
  105.6 6.6 %fusion.18 = f32[1024,1024]{1,0:T(8,128)} fusion(bf16[1024,1024]{1,0:T(8,128)(2,1)S(1)} %convolution_convert_fusion), kind=kOutput, calls=%fused_computation.33 | convolution fusion | flops 4300210176 | bytes 6291456 | tf_op jit(solution)/shard_map/dot_general | solution.py:22
  112.2 1.4 fusion.20
  114.3 1.4 copy.86
  115.7 4.1 %all-to-all-start.1 = ((bf16[32,2,64,128]{3,2,1,0:T(8,128)(2,1)}), bf16[32,2,64,128]{3,2,1,0:T(8,128)(2,1)S(1)}, u32[]{:S(2)}, u32[]{:S(2)}) async-start(bf16[32,2,64,128]{3,2,1,0:T(8,128)(2,1)} %copy.86), calls=%async_computation.1 | async-start | bytes 2097152 | tf_op jit(solution)/shard_map/all_to_all | solution.py:107
  121.0 25.0 %all-to-all-done.1 = bf16[32,2,64,128]{3,2,1,0:T(8,128)(2,1)S(1)} async-done(((bf16[32,2,64,128]{3,2,1,0:T(8,128)(2,1)}), bf16[32,2,64,128]{3,2,1,0:T(8,128)(2,1)S(1)}, u32[]{:S(2)}, u32[]{:S(2)}) %all-to-all-start.1) | async-done | bytes 1048608 | tf_op jit(solution)/shard_map/all_to_all | solution.py:107
  148.5 26.4 %all-gather.8.cloned.1.call-done = bf16[2048,256]{0,1:T(8,128)(2,1)} async-done(((bf16[512,256]{0,1:T(8,128)(2,1)}), bf16[2048,256]{0,1:T(8,128)(2,1)}) %all-gather.8.cloned.1.call-update) | async-done | bytes 1048592 | tf_op jit(solution)/shard_map/all_gather | solution.py:130
  174.9 2.6 %convolution_convert_fusion.2 = bf16[512,256]{1,0:T(8,128)(2,1)S(1)} fusion(bf16[512,2048]{0,1:T(8,128)(2,1)} %all-gather.6.cloned.1.call-done, bf16[2048,256]{0,1:T(8,128)(2,1)} %all-gather.8.cloned.1.call-done), kind=kOutput, calls=%fused_computation.26 | convolution fusion | flops 537001984 | bytes 3407872 | tf_op jit(solution)/shard_map/dot_general | solution.py:132
  177.5 1.5 collective-permute-start
  179.0 7.9 %collective-permute-done = bf16[512,256]{1,0:T(8,128)(2,1)S(1)} collective-permute-done((bf16[512,256]{1,0:T(8,128)(2,1)S(1)}, bf16[512,256]{1,0:T(8,128)(2,1)S(1)}, u32[]{:S(2)}, u32[]{:S(2)}) %collective-permute-start) | collective-permute-done | bytes 262176 | tf_op jit(solution)/shard_map/ppermute | solution.py:137
  186.9 8.5 %collective-permute-done.1 = bf16[512,256]{1,0:T(8,128)(2,1)S(1)} collective-permute-done((bf16[512,256]{1,0:T(8,128)(2,1)S(1)}, bf16[512,256]{1,0:T(8,128)(2,1)S(1)}, u32[]{:S(2)}, u32[]{:S(2)}) %collective-permute-start.1) | collective-permute-done | bytes 262176 | tf_op jit(solution)/shard_map/ppermute | solution.py:137
  196.3 7.3 %collective-permute-done.2 = bf16[512,256]{1,0:T(8,128)(2,1)S(1)} collective-permute-done((bf16[512,256]{1,0:T(8,128)(2,1)S(1)}, bf16[512,256]{1,0:T(8,128)(2,1)S(1)}, u32[]{:S(2)}, u32[]{:S(2)}) %collective-permute-start.2) | collective-permute-done | bytes 262176 | tf_op jit(solution)/shard_map/ppermute | solution.py:137
  209.4 3.4 %fusion.14 = f32[512,256]{1,0:T(8,128)} fusion(bf16[512,2048]{0,1:T(8,128)(2,1)} %all-gather.4.cloned.1.call-done, bf16[4096,256]{1,0:T(8,128)(2,1)} %constant_dynamic-update-slice_fusion, s32[]{:T(128)S(6)} %select_n.243), kind=kOutput, calls=%fused_computation.31 | convolution fusion | flops 536870912 | bytes 3670020 | tf_op jit(solution)/shard_map/dot_general | solution.py:142
  (102 shorter events, 23.9 us)
Async XLA Ops:
  12.1 1.8 copy-start.3
  16.2 8.1 %copy-start.5 = (s32[32]{0:T(128)S(1)}, s32[32]{0:T(128)}, u32[]{:S(2)}) copy-start(s32[32]{0:T(128)} %param.10) | copy-start | bytes 388
  16.2 9.6 %copy-start.4 = (s32[32,8]{0,1:T(8,128)S(1)}, s32[32,8]{0,1:T(8,128)}, u32[]{:S(2)}) copy-start(s32[32,8]{0,1:T(8,128)} %param.9) | copy-start | bytes 3076
  16.2 56.1 %all-to-all-start = ((bf16[32,2,128,128]{3,2,1,0:T(8,128)(2,1)}), bf16[32,2,128,128]{3,2,1,0:T(8,128)(2,1)S(1)}, u32[]{:S(2)}, u32[]{:S(2)}) async-start(bf16[32,2,128,128]{3,2,1,0:T(8,128)(2,1)} %copy.81), calls=%async_computation | async-start | bytes 4194304 | tf_op jit(solution)/shard_map/all_to_all | solution.py:68
  23.5 125.0 %all-gather.6.cloned.1.call-start = ((), (), s32[]{:S(2)}) async-start(), calls=%async_computation.3 | async-start | bytes 2359296 | tf_op jit(solution)/shard_map/all_gather | solution.py:133
  72.3 1.4 copy-start.1
  83.4 2.2 copy-start
  115.7 30.3 %all-to-all-start.1 = ((bf16[32,2,64,128]{3,2,1,0:T(8,128)(2,1)}), bf16[32,2,64,128]{3,2,1,0:T(8,128)(2,1)S(1)}, u32[]{:S(2)}, u32[]{:S(2)}) async-start(bf16[32,2,64,128]{3,2,1,0:T(8,128)(2,1)} %copy.86), calls=%async_computation.1 | async-start | bytes 2097152 | tf_op jit(solution)/shard_map/all_to_all | solution.py:107
  119.8 55.1 %all-gather.8.cloned.1.call-start = ((), (), s32[]{:S(2)}) async-start(), calls=%async_computation.4 | async-start | bytes 1310720 | tf_op jit(solution)/shard_map/all_gather | solution.py:130
  147.7 47.7 %copy-start.2 = (bf16[32,8,4,128]{3,1,2,0:T(8,128)(2,1)S(1)}, bf16[32,8,4,128]{3,1,2,0:T(8,128)(2,1)}, u32[]{:S(2)}) copy-start(bf16[32,8,4,128]{3,1,2,0:T(8,128)(2,1)} %copy.107) | copy-start | bytes 786436
  147.7 61.7 %all-gather.4.cloned.1.call-start = ((), (), s32[]{:S(2)}) async-start(), calls=%async_computation.2 | async-start | bytes 2359296 | tf_op jit(solution)/shard_map/all_gather | solution.py:143
  177.5 9.4 %collective-permute-start = (bf16[512,256]{1,0:T(8,128)(2,1)S(1)}, bf16[512,256]{1,0:T(8,128)(2,1)S(1)}, u32[]{:S(2)}, u32[]{:S(2)}) collective-permute-start(bf16[512,256]{1,0:T(8,128)(2,1)S(1)} %convolution_convert_fusion.2), channel_id=1, source_target_pairs={{0,8},{8,16},{16,24},{24,0},{1,9},{9,17},{17,25},{25,1},{2,10},{10... | collective-permute-start | bytes 786440 | tf_op jit(solution)/shard_map/ppermute | solution.py:137
  186.9 8.5 %collective-permute-start.1 = (bf16[512,256]{1,0:T(8,128)(2,1)S(1)}, bf16[512,256]{1,0:T(8,128)(2,1)S(1)}, u32[]{:S(2)}, u32[]{:S(2)}) collective-permute-start(bf16[512,256]{1,0:T(8,128)(2,1)S(1)} %collective-permute-done), channel_id=1, source_target_pairs={{0,8},{8,16},{16,24},{24,0},{1,9},{9,17},{17,25},{25,1},{2,10},{10... | collective-permute-start | bytes 786440 | tf_op jit(solution)/shard_map/ppermute | solution.py:137
  195.4 8.2 %collective-permute-start.2 = (bf16[512,256]{1,0:T(8,128)(2,1)S(1)}, bf16[512,256]{1,0:T(8,128)(2,1)S(1)}, u32[]{:S(2)}, u32[]{:S(2)}) collective-permute-start(bf16[512,256]{1,0:T(8,128)(2,1)S(1)} %collective-permute-done.1), channel_id=1, source_target_pairs={{0,8},{8,16},{16,24},{24,0},{1,9},{9,17},{17,25},{25,1},{2,10},{10... | collective-permute-start | bytes 786440 | tf_op jit(solution)/shard_map/ppermute | solution.py:137
Sparse Core Ops, SparseCore 0:
  26.8 35.3 all-gather.5
  147.8 26.9 all-gather.7
  177.3 27.1 all-gather.3
